TPU v7x, 512 devices: a whole 4x4x16 slice. The times are simulated.
512 devices in a mesh: fsdp: 32 (over y, z_lo, core), head: 4 (over z_hi), seq: 4 (over x).
Axes of the slice: x: 4, y: 4, z: 16 (z_hi: 4, z_lo: 4; z = z_hi * 4 + z_lo), core: 2. Of those that a mesh axis runs over, the one named last changes fastest.
Arguments:
- latents: bfloat16 [6144, 6144], P('fsdp', ('head', 'seq')), may hold values from -100 to 100
- train_qkv: bfloat16 [3, 6144, 4096], P(None, 'fsdp', ('head', 'seq')), may hold values from -0.078125 to 0.078125
- ema_qkv: bfloat16 [3, 6144, 4096], P(None, 'fsdp', ('head', 'seq')), may hold values from -0.078125 to 0.078125
- q_gain: float32 [128], replicated, may hold values from 0.8 to 2.5
- k_gain: float32 [128], replicated, may hold values from 0.8 to 2.5
- out_weight: bfloat16 [4096, 6144], P(('head', 'seq')), may hold values from -0.125 to 0.125
- modulation: float32 [8, 3, 6144], replicated, may hold values from -4 to 4
- timestep: int32 [1], replicated, may hold values from 0 to 7
- step: int32 [1], replicated, may hold values from 0 to 7
Outputs:
- block_output: bfloat16 [6144, 6144], P('fsdp', ('head', 'seq'))
All inputs are finite; a program needn't handle non-finite values.
Results may differ from a plain program's by a relative error of at most 0.025.
Values may be sent and summed in bfloat16 or wider, within the bound.
No kernel may reach another device: no remote copies, remote signals or barrier semaphores. Data moves between devices by JAX's collectives and lax.ppermute only.
A program may use at most 64 MiB of HBM per device.

v0:
```python
import math
import jax
import jax.numpy as jnp
from jax import lax
from jax.sharding import PartitionSpec as P

D = 6144
HD = 128


def head_norm(projected_part, gain, heads):
    shaped = projected_part.reshape(projected_part.shape[0], heads, HD)
    squares = jnp.mean(shaped * shaped, axis=2, keepdims=True)
    return (shaped * lax.rsqrt(squares + 1e-06) * gain).astype(jnp.bfloat16)


def per_device(latents, train_qkv, ema_qkv, q_gain, k_gain, out_weight, modulation, timestep, step):
    rows_here = latents.shape[0]
    local_width = latents.shape[1]
    channels = ema_qkv.shape[2]
    heads = channels // HD
    stepped = step[0].astype(jnp.float32)
    decay = (1.0 + stepped) / (10.0 + stepped)
    ema_weights = (
        decay * ema_qkv.astype(jnp.float32) + (1.0 - decay) * train_qkv.astype(jnp.float32)
    ).astype(jnp.bfloat16)
    chosen = (jnp.arange(modulation.shape[0], dtype=jnp.int32) == timestep[0]).astype(jnp.float32)
    mod_row = jnp.einsum("n,ncd->cd", chosen, modulation, precision=lax.Precision.HIGHEST)
    position = lax.axis_index(("head", "seq")) * local_width
    own_mod = lax.dynamic_slice_in_dim(mod_row, position, local_width, 1)
    widened = latents.astype(jnp.float32)
    average = lax.psum(jnp.sum(widened, axis=1), ("head", "seq")) / D
    centred = widened - average[:, None]
    variance = lax.psum(jnp.sum(centred * centred, axis=1), ("head", "seq")) / D
    shares = (
        centred * lax.rsqrt(variance + 1e-06)[:, None] * (1.0 + own_mod[1]) + own_mod[0]
    ).astype(jnp.bfloat16)
    hidden = lax.all_gather(shares, ("head", "seq"), axis=1, tiled=True)
    full_weights = lax.all_gather(ema_weights, "fsdp", axis=1, tiled=True)
    projected = jnp.einsum("td,jdh->jth", hidden, full_weights, preferred_element_type=jnp.float32)
    queries = head_norm(projected[0], q_gain, heads)
    keys = head_norm(projected[1], k_gain, heads).reshape(rows_here, channels)
    values = projected[2].astype(jnp.bfloat16)
    scaling = 1.0 / math.sqrt(HD)

    def one_block(carry, operands):
        numer, totals = carry
        key_block, value_block = operands
        scores = (
            jnp.einsum("qhd,khd->hqk", queries, key_block, preferred_element_type=jnp.float32)
            * scaling
        )
        expo = jnp.exp(scores)
        weights = expo.astype(jnp.bfloat16)
        numer = numer + jnp.einsum(
            "hqk,khd->qhd", weights, value_block, preferred_element_type=jnp.float32
        )
        totals = totals + jnp.transpose(jnp.sum(expo, axis=2))
        return ((numer, totals), None)

    starting_numer = jnp.zeros((rows_here, heads, HD), jnp.float32)
    starting_totals = jnp.zeros((rows_here, heads), jnp.float32)
    carry = (starting_numer, starting_totals)
    pieces = (
        lax.all_gather(keys, "fsdp", axis=0, tiled=True),
        lax.all_gather(values, "fsdp", axis=0, tiled=True),
    )
    piece_rows = pieces[0].shape[0]
    block_rows = math.gcd(piece_rows, 512)
    count = piece_rows // block_rows
    key_blocks = pieces[0].reshape(count, block_rows, heads, HD)
    value_blocks = pieces[1].reshape(count, block_rows, heads, HD)
    carry, _ = lax.scan(one_block, carry, (key_blocks, value_blocks))
    numer, totals = carry
    attended = (numer / totals[:, :, None]).astype(jnp.bfloat16).reshape(rows_here, channels)
    partial_terms = jnp.dot(attended, out_weight, preferred_element_type=jnp.float32).astype(
        jnp.bfloat16
    )
    summed = lax.psum(partial_terms, ("head", "seq")).astype(jnp.float32)
    branch = lax.dynamic_slice_in_dim(summed, position, local_width, 1)
    return (widened + own_mod[2][None, :] * branch).astype(jnp.bfloat16)


def solution(mesh):
    in_specs = (
        P("fsdp", ("head", "seq")),
        P(None, "fsdp", ("head", "seq")),
        P(None, "fsdp", ("head", "seq")),
        P(),
        P(),
        P(("head", "seq"), None),
        P(),
        P(),
        P(),
    )
    out_specs = P("fsdp", ("head", "seq"))
    return jax.shard_map(
        per_device, mesh=mesh, in_specs=in_specs, out_specs=out_specs, check_vma=False
    )
```

profile of v0, /device:TPU:40, one launch (start us, length us, event | category | flops | bytes accessed | tf_op | source)
XLA Modules:
  0.0 781.6 jit_solution(2207394032525884099)
XLA Ops:
  10.0 58.4 %psum.21 = f32[192]{0:T(256)S(1)} all-reduce(f32[192]{0:T(256)S(1)} %convert_reduce_fusion), channel_id=1, replica_groups=mesh['fsdp'=32,'head'=4,'seq'=4] {'head','seq'}, use_global_device_ids=true, to_apply=%region_1.0 | all-reduce | flops 192 | bytes 1536 | tf_op jit(solution)/shard_map/psum | solution.py:32
  69.5 46.3 %psum.22 = f32[192]{0:T(256)S(1)} all-reduce(f32[192]{0:T(256)S(1)} %fusion.11), channel_id=1, replica_groups=mesh['fsdp'=32,'head'=4,'seq'=4] {'head','seq'}, use_global_device_ids=true, to_apply=%region_3.0 | all-reduce | flops 192 | bytes 1536 | tf_op jit(solution)/shard_map/psum | solution.py:34
  121.0 85.2 %all-gather.8.cloned.1.call-done = bf16[192,6144]{1,0:T(8,128)(2,1)} async-done(((bf16[192,384]{1,0:T(8,128)(2,1)}), bf16[192,6144]{1,0:T(8,128)(2,1)}) %all-gather.8.cloned.1.call-update) | async-done | bytes 2359312 | tf_op jit(solution)/shard_map/all_gather | solution.py:38
  206.2 81.8 %all-gather.6.cloned.1.call-done = bf16[3,6144,256]{2,1,0:T(8,128)(2,1)} async-done(((bf16[3,192,256]{2,1,0:T(8,128)(2,1)}), bf16[3,6144,256]{2,1,0:T(8,128)(2,1)}) %all-gather.6.cloned.1.call-update) | async-done | bytes 9437200 | tf_op jit(solution)/shard_map/all_gather | solution.py:39
  287.9 6.4 fusion.6
  302.9 63.6 %all-gather.10.cloned.1.call-done = bf16[6144,256]{1,0:T(8,128)(2,1)} async-done(((bf16[192,256]{1,0:T(8,128)(2,1)}), bf16[6144,256]{1,0:T(8,128)(2,1)}) %all-gather.10.cloned.1.call-update) | async-done | bytes 3145744 | tf_op jit(solution)/shard_map/all_gather | solution.py:65
  366.5 5.5 reshape.43
  372.0 62.2 %all-gather.12.cloned.1.call-done = bf16[1,6144,256]{2,1,0:T(8,128)(2,1)} async-done(((bf16[1,192,256]{2,1,0:T(8,128)(2,1)}), bf16[1,6144,256]{2,1,0:T(8,128)(2,1)}) %all-gather.12.cloned.1.call-update) | async-done | bytes 3145744 | tf_op jit(solution)/shard_map/all_gather | solution.py:66
  434.2 5.5 reshape.42
  439.7 53.4 %while.13 = (s32[]{:T(128)}, f32[192,2,128]{2,0,1:T(8,128)}, f32[192,2]{0,1:T(2,128)S(1)}, bf16[12,512,2,128]{3,2,1,0:T(2,128)(2,1)}, bf16[12,512,2,128]{3,2,1,0...) while((s32[]{:T(128)}, f32[192,2,128]{2,0,1:T(8,128)}, ...), condition=%wide.region_8.9_spmd.clone, body=%wide.region_6.8_spmd.clone.sunk | while | flops 101351808 | bytes 2857060 | solution.py:73
  442.2 1.9 fusion.45
  446.6 2.0 fusion.45
  451.0 2.0 fusion.45
  455.5 2.0 fusion.45
  459.9 2.0 fusion.45
  464.4 2.0 fusion.45
  468.9 2.0 fusion.45
  473.3 2.0 fusion.45
  477.8 2.0 fusion.45
  482.2 2.0 fusion.45
  486.7 2.0 fusion.45
  491.1 2.0 fusion.45
  493.1 3.2 convolution_convert_fusion
  496.4 277.0 %all-reduce.2.cloned.1.call-done = bf16[192,6144]{1,0:T(8,128)(2,1)} async-done(((bf16[192,6144]{1,0:T(8,128)(2,1)}), bf16[192,6144]{1,0:T(8,128)(2,1)}) %all-reduce.2.cloned.1.call-update) | async-done | bytes 2359312 | tf_op jit(solution)/shard_map/psum | solution.py:79
  (79 shorter events, 47.9 us)
Async XLA Ops:
  6.5 486.6 %copy-start = (bf16[256,6144]{1,0:T(8,128)(2,1)S(1)}, bf16[256,6144]{1,0:T(8,128)(2,1)}, u32[]{:S(2)}) copy-start(bf16[256,6144]{1,0:T(8,128)(2,1)} %param.16) | copy-start | bytes 9437188
  6.5 199.6 %all-gather.8.cloned.1.call-start = ((), (), s32[]{:S(2)}) async-start(), calls=%async_computation.1 | async-start | bytes 2506752 | tf_op jit(solution)/shard_map/all_gather | solution.py:38
  117.6 170.3 %all-gather.6.cloned.1.call-start = ((), (), s32[]{:S(2)}) async-start(), calls=%async_computation | async-start | bytes 9732096 | tf_op jit(solution)/shard_map/all_gather | solution.py:39
  120.3 246.2 %all-gather.10.cloned.1.call-start = ((), (), s32[]{:S(2)}) async-start(), calls=%async_computation.2 | async-start | bytes 3244032 | tf_op jit(solution)/shard_map/all_gather | solution.py:65
  294.3 0.8 copy-start.2
  295.1 7.7 copy-start.3
  300.6 133.7 %all-gather.12.cloned.1.call-start = ((), (), s32[]{:S(2)}) async-start(), calls=%async_computation.4 | async-start | bytes 3244032 | tf_op jit(solution)/shard_map/all_gather | solution.py:66
  302.2 471.2 %all-reduce.2.cloned.1.call-start = ((), (), s32[]{:S(2)}) async-start(), calls=%async_computation.3 | async-start | bytes 4718592 | tf_op jit(solution)/shard_map/psum | solution.py:79
  493.1 280.3 %copy-start.1 = (bf16[192,384]{1,0:T(8,128)(2,1)S(1)}, bf16[192,384]{1,0:T(8,128)(2,1)}, u32[]{:S(2)}) copy-start(bf16[192,384]{1,0:T(8,128)(2,1)} %param.11) | copy-start | bytes 442372
Sparse Core Ops, SparseCore 0:
  117.7 88.3 all-gather.7
  208.2 79.6 all-gather.5
  300.7 65.7 all-gather.9
  368.5 65.7 all-gather.11
  496.5 276.8 all-reduce.1
where the time goes:
time: 783 us; the launch traced here: 782 us
  waiting for transfers between devices  570 us (73%)
  blocking collectives  105 us (13%)
  matrix products  47.8 us (6%)
  local copies, waits for them, and re-layouts  32.3 us (4%)
  between operations  14.7 us (2%)
  other arithmetic  12.1 us (2%)
    psum x1, waiting for transfers between devices, per_device(): summed = lax.psum(partial_terms, ('head', 'seq')).astype(jnp.float32)  277 us
    all_gather x1, waiting for transfers between devices, per_device(): hidden = lax.all_gather(shares, ('head', 'seq'), axis=1, tiled=True)  85.2 us
    all_gather x1, waiting for transfers between devices, per_device(): full_weights = lax.all_gather(ema_weights, 'fsdp', axis=1, tiled=True)  81.8 us
    all_gather x1, waiting for transfers between devices, per_device(): lax.all_gather(keys, 'fsdp', axis=0, tiled=True)  63.6 us
    all_gather x1, waiting for transfers between devices, per_device(): lax.all_gather(values, 'fsdp', axis=0, tiled=True)  62.2 us
    psum x1, blocking collectives, per_device(): average = lax.psum(jnp.sum(widened, axis=1), ('head', 'seq')) / D  58.4 us
    psum x1, blocking collectives, per_device(): variance = lax.psum(jnp.sum(centred * centred, axis=1), ('head', 'seq')) / D  46.3 us
    dot_general x12, matrix products, one_block(): jnp.einsum('hqk,khd->qhd', weights, value_block, preferred_element_type=j...  23.8 us
  transfers between devices with their start and end apart: 5, of which 5 were waited for; matrix products, arithmetic and copies ran while one was open for 1% of the time, Pallas kernels for 0%

commit v1 on v0

--- a/solution.py
+++ b/solution.py
@@ -29,7 +29,7 @@
     position = lax.axis_index(("head", "seq")) * local_width
     own_mod = lax.dynamic_slice_in_dim(mod_row, position, local_width, 1)
     widened = latents.astype(jnp.float32)
-    average = lax.psum(jnp.sum(widened, axis=1), ("head", "seq")) / D
+    average = lax.psum(lax.psum(jnp.sum(widened, axis=1), "seq"), "head") / D
     centred = widened - average[:, None]
     variance = lax.psum(jnp.sum(centred * centred, axis=1), ("head", "seq")) / D
     shares = (

time: 783 us -> 757 us (0.967)
  blocking collectives: 105 us -> 79.8 us
    psum x1 -> x2, blocking collectives: 58.4 us -> 30.8 us  [per_device(): average = lax.psum(lax.psum(jnp.sum(widened, axis=1), 'seq'), 'head') / D]
where the time goes in v1:
time: 757 us; the launch traced here: 756 us
  waiting for transfers between devices  569 us (75%)
  blocking collectives  79.8 us (11%)
  matrix products  47.8 us (6%)
  local copies, waits for them, and re-layouts  32.3 us (4%)
  between operations  14.7 us (2%)
  other arithmetic  12.1 us (2%)
    psum x1, waiting for transfers between devices, per_device(): summed = lax.psum(partial_terms, ('head', 'seq')).astype(jnp.float32)  276 us
    all_gather x1, waiting for transfers between devices, per_device(): hidden = lax.all_gather(shares, ('head', 'seq'), axis=1, tiled=True)  85.4 us
    all_gather x1, waiting for transfers between devices, per_device(): full_weights = lax.all_gather(ema_weights, 'fsdp', axis=1, tiled=True)  81.8 us
    all_gather x1, waiting for transfers between devices, per_device(): lax.all_gather(keys, 'fsdp', axis=0, tiled=True)  63.5 us
    all_gather x1, waiting for transfers between devices, per_device(): lax.all_gather(values, 'fsdp', axis=0, tiled=True)  62.2 us
    psum x1, blocking collectives, per_device(): variance = lax.psum(jnp.sum(centred * centred, axis=1), ('head', 'seq')) / D  49 us
    psum x2, blocking collectives, per_device(): average = lax.psum(lax.psum(jnp.sum(widened, axis=1), 'seq'), 'head') / D  30.8 us
    dot_general x12, matrix products, one_block(): jnp.einsum('hqk,khd->qhd', weights, value_block, preferred_element_type=j...  23.8 us
  transfers between devices with their start and end apart: 5, of which 5 were waited for; matrix products, arithmetic and copies ran while one was open for 1% of the time, Pallas kernels for 0%

profile of v1, /device:TPU:40, one launch (start us, length us, event | category | flops | bytes accessed | tf_op | source)
XLA Modules:
  0.0 756.3 jit_solution(6647870491873004011)
XLA Ops:
  10.0 10.5 %psum.28 = f32[192]{0:T(256)S(1)} all-reduce(f32[192]{0:T(256)S(1)} %convert_reduce_fusion), channel_id=1, replica_groups=mesh['fsdp'=32,'head'=4,'seq'=4] {'seq'}, use_global_device_ids=true, to_apply=%region_1.0 | all-reduce | flops 192 | bytes 1536 | tf_op jit(solution)/shard_map/psum | solution.py:32
  20.5 20.3 %psum.29 = f32[192]{0:T(256)S(1)} all-reduce(f32[192]{0:T(256)S(1)} %psum.28), channel_id=1, replica_groups=mesh['fsdp'=32,'head'=4,'seq'=4] {'head'}, use_global_device_ids=true, to_apply=%region_2.0 | all-reduce | flops 192 | bytes 1536 | tf_op jit(solution)/shard_map/psum | solution.py:32
  42.0 49.0 %psum.30 = f32[192]{0:T(256)S(1)} all-reduce(f32[192]{0:T(256)S(1)} %fusion.11), channel_id=1, replica_groups=mesh['fsdp'=32,'head'=4,'seq'=4] {'head','seq'}, use_global_device_ids=true, to_apply=%region_4.0 | all-reduce | flops 192 | bytes 1536 | tf_op jit(solution)/shard_map/psum | solution.py:34
  96.1 85.4 %all-gather.8.cloned.1.call-done = bf16[192,6144]{1,0:T(8,128)(2,1)} async-done(((bf16[192,384]{1,0:T(8,128)(2,1)}), bf16[192,6144]{1,0:T(8,128)(2,1)}) %all-gather.8.cloned.1.call-update) | async-done | bytes 2359312 | tf_op jit(solution)/shard_map/all_gather | solution.py:38
  181.6 81.8 %all-gather.6.cloned.1.call-done = bf16[3,6144,256]{2,1,0:T(8,128)(2,1)} async-done(((bf16[3,192,256]{2,1,0:T(8,128)(2,1)}), bf16[3,6144,256]{2,1,0:T(8,128)(2,1)}) %all-gather.6.cloned.1.call-update) | async-done | bytes 9437200 | tf_op jit(solution)/shard_map/all_gather | solution.py:39
  263.3 6.4 fusion.6
  278.3 63.5 %all-gather.10.cloned.1.call-done = bf16[6144,256]{1,0:T(8,128)(2,1)} async-done(((bf16[192,256]{1,0:T(8,128)(2,1)}), bf16[6144,256]{1,0:T(8,128)(2,1)}) %all-gather.10.cloned.1.call-update) | async-done | bytes 3145744 | tf_op jit(solution)/shard_map/all_gather | solution.py:65
  341.9 5.5 reshape.43
  347.4 62.2 %all-gather.12.cloned.1.call-done = bf16[1,6144,256]{2,1,0:T(8,128)(2,1)} async-done(((bf16[1,192,256]{2,1,0:T(8,128)(2,1)}), bf16[1,6144,256]{2,1,0:T(8,128)(2,1)}) %all-gather.12.cloned.1.call-update) | async-done | bytes 3145744 | tf_op jit(solution)/shard_map/all_gather | solution.py:66
  409.7 5.5 reshape.42
  415.2 53.4 %while.13 = (s32[]{:T(128)}, f32[192,2,128]{2,0,1:T(8,128)}, f32[192,2]{0,1:T(2,128)S(1)}, bf16[12,512,2,128]{3,2,1,0:T(2,128)(2,1)}, bf16[12,512,2,128]{3,2,1,0...) while((s32[]{:T(128)}, f32[192,2,128]{2,0,1:T(8,128)}, ...), condition=%wide.region_9.10_spmd.clone, body=%wide.region_7.9_spmd.clone.sunk | while | flops 101351808 | bytes 2857060 | solution.py:73
  422.0 2.0 fusion.45
  426.5 2.0 fusion.45
  430.9 2.0 fusion.45
  435.4 2.0 fusion.45
  439.8 2.0 fusion.45
  444.3 2.0 fusion.45
  448.8 2.0 fusion.45
  453.2 2.0 fusion.45
  457.7 2.0 fusion.45
  462.1 2.0 fusion.45
  466.6 2.0 fusion.45
  468.6 3.2 convolution_convert_fusion
  471.8 276.3 %all-reduce.2.cloned.1.call-done = bf16[192,6144]{1,0:T(8,128)(2,1)} async-done(((bf16[192,6144]{1,0:T(8,128)(2,1)}), bf16[192,6144]{1,0:T(8,128)(2,1)}) %all-reduce.2.cloned.1.call-update) | async-done | bytes 2359312 | tf_op jit(solution)/shard_map/psum | solution.py:79
  (80 shorter events, 49.8 us)
Async XLA Ops:
  6.5 462.0 %copy-start = (bf16[256,6144]{1,0:T(8,128)(2,1)S(1)}, bf16[256,6144]{1,0:T(8,128)(2,1)}, u32[]{:S(2)}) copy-start(bf16[256,6144]{1,0:T(8,128)(2,1)} %param.16) | copy-start | bytes 9437188
  6.5 175.0 %all-gather.8.cloned.1.call-start = ((), (), s32[]{:S(2)}) async-start(), calls=%async_computation.1 | async-start | bytes 2506752 | tf_op jit(solution)/shard_map/all_gather | solution.py:38
  92.8 170.5 %all-gather.6.cloned.1.call-start = ((), (), s32[]{:S(2)}) async-start(), calls=%async_computation | async-start | bytes 9732096 | tf_op jit(solution)/shard_map/all_gather | solution.py:39
  95.4 246.5 %all-gather.10.cloned.1.call-start = ((), (), s32[]{:S(2)}) async-start(), calls=%async_computation.2 | async-start | bytes 3244032 | tf_op jit(solution)/shard_map/all_gather | solution.py:65
  269.7 0.8 copy-start.2
  270.5 7.7 %copy-start.3 = (f32[128]{0:T(128)S(1)}, f32[128]{0:T(128)}, u32[]{:S(2)}) copy-start(f32[128]{0:T(128)} %param.14) | copy-start | bytes 1540
  276.0 133.7 %all-gather.12.cloned.1.call-start = ((), (), s32[]{:S(2)}) async-start(), calls=%async_computation.4 | async-start | bytes 3244032 | tf_op jit(solution)/shard_map/all_gather | solution.py:66
  277.7 470.5 %all-reduce.2.cloned.1.call-start = ((), (), s32[]{:S(2)}) async-start(), calls=%async_computation.3 | async-start | bytes 4718592 | tf_op jit(solution)/shard_map/psum | solution.py:79
  468.6 279.6 %copy-start.1 = (bf16[192,384]{1,0:T(8,128)(2,1)S(1)}, bf16[192,384]{1,0:T(8,128)(2,1)}, u32[]{:S(2)}) copy-start(bf16[192,384]{1,0:T(8,128)(2,1)} %param.11) | copy-start | bytes 442372
Sparse Core Ops, SparseCore 0:
  92.9 88.6 all-gather.7
  183.7 79.6 all-gather.5
  276.1 65.7 all-gather.9
  343.9 65.7 all-gather.11
  471.9 276.1 all-reduce.1

commit v2 on v0

--- a/solution.py
+++ b/solution.py
@@ -76,7 +76,7 @@
     partial_terms = jnp.dot(attended, out_weight, preferred_element_type=jnp.float32).astype(
         jnp.bfloat16
     )
-    summed = lax.psum(partial_terms, ("head", "seq")).astype(jnp.float32)
+    summed = jnp.sum(lax.all_gather(partial_terms, ("head", "seq")), axis=0).astype(jnp.float32)
     branch = lax.dynamic_slice_in_dim(summed, position, local_width, 1)
     return (widened + own_mod[2][None, :] * branch).astype(jnp.bfloat16)
 

time: 783 us -> 1300 us (1.66)
  the two profiles are of different devices: /device:TPU:40 before, /device:TPU:1 now
where the time goes in v2:
time: 1300 us
  waiting for transfers between devices  1120 us (86%)
  blocking collectives  92.2 us (7%)
  local copies, waits for them, and re-layouts  31.6 us (2%)
  other arithmetic  27.7 us (2%)
  matrix products  18.1 us (1%)
  between operations  14.8 us (1%)
    all_gather x1, waiting for transfers between devices, per_device(): lax.all_gather(partial_terms, ('head', 'seq'))  812 us
    all_gather x1, waiting for transfers between devices, per_device(): hidden = lax.all_gather(shares, ('head', 'seq'), axis=1, tiled=True)  108 us
    all_gather x1, waiting for transfers between devices, per_device(): full_weights = lax.all_gather(ema_weights, 'fsdp', axis=1, tiled=True)  75 us
    all_gather x1, waiting for transfers between devices, per_device(): lax.all_gather(keys, 'fsdp', axis=0, tiled=True)  62.1 us
    all_gather x1, waiting for transfers between devices, per_device(): lax.all_gather(values, 'fsdp', axis=0, tiled=True)  58.2 us
    psum x1, blocking collectives, per_device(): average = lax.psum(jnp.sum(widened, axis=1), ('head', 'seq')) / D  52.9 us
    psum x1, blocking collectives, per_device(): variance = lax.psum(jnp.sum(centred * centred, axis=1), ('head', 'seq')) / D  39.3 us
  transfers between devices with their start and end apart: 5, of which 5 were waited for; matrix products, arithmetic and copies ran while one was open for 1% of the time, Pallas kernels for 0%

profile of v2, /device:TPU:1, one launch (start us, length us, event | category | flops | bytes accessed | tf_op | source)
XLA Modules:
  0.0 1300.0 jit_solution(17180881695900988566)
XLA Ops:
  8.5 52.9 %psum.14 = f32[192]{0:T(256)S(1)} all-reduce(f32[192]{0:T(256)S(1)} %convert_reduce_fusion), channel_id=1, replica_groups=mesh['fsdp'=32,'head'=4,'seq'=4] {'head','seq'}, use_global_device_ids=true, to_apply=%region_1.0 | all-reduce | flops 192 | bytes 1536 | tf_op jit(solution)/shard_map/psum | solution.py:32
  62.5 39.3 %psum.15 = f32[192]{0:T(256)S(1)} all-reduce(f32[192]{0:T(256)S(1)} %fusion.11), channel_id=1, replica_groups=mesh['fsdp'=32,'head'=4,'seq'=4] {'head','seq'}, use_global_device_ids=true, to_apply=%region_3.0 | all-reduce | flops 192 | bytes 1536 | tf_op jit(solution)/shard_map/psum | solution.py:34
  101.8 1.5 fusion.23
  103.4 1.7 fusion.14
  105.9 1.9 add_convert_fusion
  107.9 107.7 %all-gather.10.cloned.1.call-done = bf16[192,6144]{1,0:T(8,128)(2,1)} async-done(((bf16[192,384]{1,0:T(8,128)(2,1)}), bf16[192,6144]{1,0:T(8,128)(2,1)}) %all-gather.10.cloned.1.call-update) | async-done | bytes 2359312 | tf_op jit(solution)/shard_map/all_gather | solution.py:38
  215.6 75.0 %all-gather.8.cloned.1.call-done = bf16[3,6144,256]{2,1,0:T(8,128)(2,1)} async-done(((bf16[3,192,256]{2,1,0:T(8,128)(2,1)}), bf16[3,6144,256]{2,1,0:T(8,128)(2,1)}) %all-gather.8.cloned.1.call-update) | async-done | bytes 9437200 | tf_op jit(solution)/shard_map/all_gather | solution.py:39
  290.6 6.4 fusion.6
  298.6 1.7 fusion.30
  301.0 1.6 fusion.17
  306.3 58.2 %all-gather.14.cloned.1.call-done = bf16[1,6144,256]{2,1,0:T(8,128)(2,1)} async-done(((bf16[1,192,256]{2,1,0:T(8,128)(2,1)}), bf16[1,6144,256]{2,1,0:T(8,128)(2,1)}) %all-gather.14.cloned.1.call-update) | async-done | bytes 3145744 | tf_op jit(solution)/shard_map/all_gather | solution.py:66
  364.5 5.5 reshape.42
  370.0 62.1 %all-gather.12.cloned.1.call-done = bf16[6144,256]{1,0:T(8,128)(2,1)} async-done(((bf16[192,256]{1,0:T(8,128)(2,1)}), bf16[6144,256]{1,0:T(8,128)(2,1)}) %all-gather.12.cloned.1.call-update) | async-done | bytes 3145744 | tf_op jit(solution)/shard_map/all_gather | solution.py:65
  432.2 5.5 reshape.43
  437.7 25.2 %while.13 = (s32[]{:T(128)}, f32[192,2,128]{2,0,1:T(8,128)S(1)}, f32[192,2]{0,1:T(2,128)S(1)}, bf16[12,512,2,128]{3,2,1,0:T(2,128)(2,1)}, bf16[12,512,2,128]{3,2...) while((s32[]{:T(128)}, f32[192,2,128]{2,0,1:T(8,128)S(1)}, ...), condition=%wide.region_8.9_spmd.clone, body=%wide.region_6.8_spmd.clone.sunk | while | flops 101351808 | bytes 2857068 | solution.py:73
  441.9 1.4 constant_dynamic-slice_fusion.3
  444.0 1.4 constant_dynamic-slice_fusion.3
  446.1 1.4 constant_dynamic-slice_fusion.3
  450.3 1.4 constant_dynamic-slice_fusion.3
  452.4 1.4 constant_dynamic-slice_fusion.3
  462.9 2.2 convolution_convert_fusion
  465.2 812.0 %all-gather.16.cloned.1.call-done = bf16[3072,6144]{1,0:T(8,128)(2,1)} async-done(((bf16[192,6144]{1,0:T(8,128)(2,1)}), bf16[3072,6144]{1,0:T(8,128)(2,1)}) %all-gather.16.cloned.1.call-update) | async-done | bytes 37748752 | tf_op jit(solution)/shard_map/all_gather | solution.py:79
  1277.2 14.7 %reduce_sum.61 = bf16[192,6144]{1,0:T(8,128)(2,1)} reduce(bf16[16,192,6144]{2,1,0:T(8,128)(2,1)} %bitcast.68, bf16[]{:T(256)} %constant.51.clone.1), dimensions={0}, to_apply=%region_9.10 | reduce | flops 17694720 | bytes 40108032 | tf_op jit(solution)/shard_map/reduce_sum | solution.py:79
  1291.9 1.6 fusion.15
  (86 shorter events, 26.4 us)
Async XLA Ops:
  6.5 456.4 %copy-start = (bf16[256,6144]{1,0:T(8,128)(2,1)S(1)}, bf16[256,6144]{1,0:T(8,128)(2,1)}, u32[]{:S(2)}) copy-start(bf16[256,6144]{1,0:T(8,128)(2,1)} %param.16) | copy-start | bytes 9437188
  6.5 209.0 %all-gather.10.cloned.1.call-start = ((), (), s32[]{:S(2)}) async-start(), calls=%async_computation.1 | async-start | bytes 2506752 | tf_op jit(solution)/shard_map/all_gather | solution.py:38
  105.2 185.4 %all-gather.8.cloned.1.call-start = ((), (), s32[]{:S(2)}) async-start(), calls=%async_computation | async-start | bytes 9732096 | tf_op jit(solution)/shard_map/all_gather | solution.py:39
  107.8 190.7 %copy-start.6 = (f32[128]{0:T(128)S(1)}, f32[128]{0:T(128)}, u32[]{:S(2)}) copy-start(f32[128]{0:T(128)} %param.15) | copy-start | bytes 1540
  107.8 256.7 %all-gather.14.cloned.1.call-start = ((), (), s32[]{:S(2)}) async-start(), calls=%async_computation.3 | async-start | bytes 3244032 | tf_op jit(solution)/shard_map/all_gather | solution.py:66
  297.0 0.8 copy-start.3
  297.8 7.8 copy-start.5
  298.5 133.7 %all-gather.12.cloned.1.call-start = ((), (), s32[]{:S(2)}) async-start(), calls=%async_computation.2 | async-start | bytes 3244032 | tf_op jit(solution)/shard_map/all_gather | solution.py:65
  302.6 974.6 %all-gather.16.cloned.1.call-start = ((), (), s32[]{:S(2)}) async-start(), calls=%async_computation.4 | async-start | bytes 40108032 | tf_op jit(solution)/shard_map/all_gather | solution.py:79
  370.0 67.7 %copy-start.4 = (bf16[192,2,128]{2,0,1:T(8,128)(2,1)S(1)}, bf16[192,2,128]{2,0,1:T(8,128)(2,1)}, u32[]{:S(2)}) copy-start(bf16[192,2,128]{2,0,1:T(8,128)(2,1)} %fusion.19) | copy-start | bytes 294916
  1277.2 14.7 %copy-start.2 = (bf16[192,384]{1,0:T(8,128)(2,1)S(1)}, bf16[192,384]{1,0:T(8,128)(2,1)}, u32[]{:S(2)}) copy-start(bf16[192,384]{1,0:T(8,128)(2,1)} %param.11) | copy-start | bytes 442372
  1277.2 16.3 %copy-start.1 = (bf16[256,6144]{1,0:T(8,128)(2,1)S(1)}, bf16[256,6144]{1,0:T(8,128)(2,1)}, u32[]{:S(2)}) copy-start(bf16[256,6144]{1,0:T(8,128)(2,1)} %param.16) | copy-start | bytes 9437188
Sparse Core Ops, SparseCore 0:
  105.3 110.2 all-gather.9
  217.7 72.8 all-gather.7
  298.6 65.8 all-gather.13
  366.5 65.6 all-gather.11
  465.3 811.8 all-gather.15
